TPU v7x, 32 devices: a whole 2x2x4 slice. The times are simulated.
32 devices in a mesh: section: 4 (over y, core), seq: 4 (over z), tp: 2 (over x).
Axes of the slice: x: 2, y: 2, z: 4, core: 2. Of those that a mesh axis runs over, the one named last changes fastest.
Arguments:
- queries: bfloat16 [768, 4096], P('seq', 'tp'), may hold values from -45 to 45
- keys: bfloat16 [64, 4096], P(('section', 'seq'), 'tp'), may hold values from -6 to 6
- values: bfloat16 [64, 4096], P(('section', 'seq'), 'tp'), may hold values from -6 to 6
- out_grad: bfloat16 [768, 4096], P('seq', 'tp'), may hold values from -48 to 48
- text_len: int32 [2], replicated, may hold values from 192 to 384, as said below
- key_len: int32 [4], replicated, may hold values from 8 to 16, as said below
Outputs:
- query_grad: bfloat16 [768, 4096], P('seq', 'tp')
- key_grad: float32 [64, 4096], P(('section', 'seq'), 'tp')
- value_grad: float32 [64, 4096], P(('section', 'seq'), 'tp')
Inputs may be any that keep to these rules, and one draw needn't show every extreme that they name: `text_len`: one length per report sequence of 384 rows; rows at or past it are padding. `key_len`: live volume tokens of each slab of 16; the slab's later tokens are padding.
All inputs are finite; a program needn't handle non-finite values.
Results may differ from a plain program's by a relative error of at most 0.009.
Values may be sent and summed in bfloat16 or wider, within the bound.
A program may use at most 64 MiB of HBM per device.

v0:
```python
import math

import jax
import jax.numpy as jnp
from jax import lax
from jax.sharding import PartitionSpec as P

HD = 128
SEQS = 2


def joined(x, axis, combine):
    everything = jax.tree.map(lambda part: lax.all_gather(part, axis), x)
    initial = jax.tree.map(lambda part: part[0], everything)

    def hop(k, so_far):
        return combine(so_far, jax.tree.map(lambda part: part[k], everything))

    return lax.fori_loop(1, lax.axis_size(axis), hop, initial)


def combine_full(left_part, right_part):
    top = jnp.maximum(left_part[0], right_part[0])
    left_factor = jnp.exp(left_part[0] - top)
    right_factor = jnp.exp(right_part[0] - top)
    total = left_part[1] * left_factor + right_part[1] * right_factor
    merged = left_part[2] * left_factor[..., None] + right_part[2] * right_factor[..., None]
    return (top, total, merged)


def per_device(queries, keys, values, out_grad, text_len, key_len):
    score_scale = 1.0 / math.sqrt(HD)
    row_count = queries.shape[0]
    feat_width = queries.shape[1]
    head_count = feat_width // HD
    length_rows = row_count * lax.axis_size("seq") // SEQS
    position = lax.axis_index("seq") * row_count + jnp.arange(row_count, dtype=jnp.int32)
    seq_ids = position // length_rows
    limits = jnp.sum(
        jnp.where(
            seq_ids[:, None] == jnp.arange(SEQS, dtype=jnp.int32)[None, :], text_len[None, :], 0
        ),
        axis=1,
    )
    masked_grad = jnp.where(
        (position % length_rows < limits)[:, None], out_grad, jnp.zeros_like(out_grad)
    )
    slab_index = lax.axis_index("section")
    live_count = jnp.sum(
        jnp.where(jnp.arange(key_len.shape[0], dtype=jnp.int32) == slab_index, key_len, 0)
    )
    key_all, value_all = (
        lax.all_gather(keys, "seq", axis=0, tiled=True),
        lax.all_gather(values, "seq", axis=0, tiled=True),
    )
    key_total = key_all.shape[0]
    query_heads = queries.reshape(row_count, head_count, HD)
    grad_heads = masked_grad.reshape(row_count, head_count, HD)
    key_heads = key_all.reshape(key_total, head_count, HD)
    value_heads = value_all.reshape(key_total, head_count, HD)
    scores = (
        jnp.einsum("qhd,khd->qhk", query_heads, key_heads, preferred_element_type=jnp.float32)
        * score_scale
    )
    key_live = jnp.arange(key_total, dtype=jnp.int32) < live_count
    scores = jnp.where(key_live[None, None, :], scores, jnp.float32(-1e30))
    local_max = jnp.max(scores, axis=-1)
    expo = jnp.exp(scores - local_max[..., None])
    local_total = jnp.sum(expo, axis=-1)
    weighted = jnp.einsum(
        "qhk,khd->qhd", expo.astype(jnp.bfloat16), value_heads, preferred_element_type=jnp.float32
    )
    row_max, total, merged = joined((local_max, local_total, weighted), "section", combine_full)
    row_dot = jnp.sum(grad_heads * (merged / total[..., None]), axis=-1)
    probs = jnp.exp(scores - row_max[..., None]) / total[..., None]
    probs_low = probs.astype(jnp.bfloat16)
    prob_grad = jnp.einsum(
        "qhd,khd->qhk", grad_heads, value_heads, preferred_element_type=jnp.float32
    )
    score_grad = (probs * (prob_grad - row_dot[..., None])).astype(jnp.bfloat16)
    query_share = (
        jnp.einsum("qhk,khd->qhd", score_grad, key_heads, preferred_element_type=jnp.float32)
        * score_scale
    )
    query_grad = lax.psum(
        query_share.reshape(row_count, feat_width).astype(jnp.bfloat16), "section"
    )
    term_rows = lax.axis_size("seq") * keys.shape[0]
    key_term = (
        jnp.einsum("qhk,qhd->khd", score_grad, query_heads, preferred_element_type=jnp.float32)
        * score_scale
    )
    value_term = jnp.einsum(
        "qhk,qhd->khd", probs_low, grad_heads, preferred_element_type=jnp.float32
    )
    summed = lax.psum_scatter(
        jnp.stack(
            [key_term.reshape(term_rows, feat_width), value_term.reshape(term_rows, feat_width)],
            axis=1,
        ),
        "seq",
        scatter_dimension=0,
        tiled=True,
    )
    return (query_grad, summed[:, 0], summed[:, 1])


def solution(mesh):
    in_specs = (
        P("seq", "tp"),
        P(("section", "seq"), "tp"),
        P(("section", "seq"), "tp"),
        P("seq", "tp"),
        P(),
        P(),
    )
    out_specs = (P("seq", "tp"), P(("section", "seq"), "tp"), P(("section", "seq"), "tp"))
    return jax.shard_map(
        per_device, mesh=mesh, in_specs=in_specs, out_specs=out_specs, check_vma=False
    )
```

profile of v0, /device:TPU:0, one launch (start us, length us, event | category | flops | bytes accessed | tf_op | source)
XLA Modules:
  0.0 193.0 jit_solution(14795662915115848886)
XLA Ops:
  7.2 0.0 copy-start
  7.2 0.0 all-gather.9.cloned.1.call-start
  7.2 15.3 %all-gather.3 = bf16[4,4,2048]{2,1,0:T(4,128)(2,1)S(1)} all-gather(bf16[1,4,2048]{2,1,0:T(4,128)(2,1)} %bitcast.88), channel_id=1, replica_groups=mesh['section'=4,'seq'=4,'tp'=2] {'seq'}, dimensions={0}, use_global_device_ids=true | all-gather | bytes 81920 | tf_op jit(solution)/shard_map/all_gather | solution.py:53
  22.6 1.3 fusion.34
  23.8 0.6 iota_compare_fusion
  24.5 13.5 %all-gather.6 = bf16[4,4,2048]{2,1,0:T(4,128)(2,1)S(1)} all-gather(bf16[1,4,2048]{2,1,0:T(4,128)(2,1)} %bitcast.89), channel_id=1, replica_groups=mesh['section'=4,'seq'=4,'tp'=2] {'seq'}, dimensions={0}, use_global_device_ids=true | all-gather | bytes 81920 | tf_op jit(solution)/shard_map/all_gather | solution.py:54
  38.1 0.0 copy-done
  38.1 0.0 copy-start.4
  38.1 0.5 fusion.36
  38.7 0.0 copy-start.1
  38.7 0.0 copy-start.6
  38.7 0.0 copy-start.2
  38.7 1.6 convolution_bitcast_fusion
  40.3 0.0 all-gather.9.cloned.1.call-update
  40.3 0.0 copy-done.4
  40.3 0.0 all-reduce.6.cloned.1.call-start
  40.4 0.0 copy-done.6
  40.4 0.1 fusion.30
  40.5 0.0 copy-done.2
  40.5 1.1 fusion.20
  41.6 0.2 copy.74
  41.7 0.1 fusion.22
  41.8 5.2 %all-gather.5 = f32[4,192,16]{1,2,0:T(8,128)S(1)} all-gather(f32[1,192,16]{1,2,0:T(8,128)S(1)} %bitcast.87), channel_id=3, replica_groups=mesh['section'=4,'seq'=4,'tp'=2] {'section'}, dimensions={0}, use_global_device_ids=true | all-gather | bytes 61440 | tf_op jit(solution)/shard_map/all_gather | solution.py:13
  47.1 5.7 %all-gather.4 = f32[4,192,16]{1,2,0:T(8,128)} all-gather(f32[1,192,16]{1,2,0:T(8,128)S(1)} %bitcast.86), channel_id=2, replica_groups=mesh['section'=4,'seq'=4,'tp'=2] {'section'}, dimensions={0}, use_global_device_ids=true | all-gather | bytes 61440 | tf_op jit(solution)/shard_map/all_gather | solution.py:13
  52.7 0.7 slice_bitcast_fusion.1
  53.4 34.3 %all-gather.9.cloned.1.call-done = f32[768,16,128]{2,0,1:T(8,128)} async-done(((f32[192,16,128]{2,0,1:T(8,128)}), f32[768,16,128]{2,0,1:T(8,128)}) %all-gather.9.cloned.1.call-update) | async-done | bytes 6291472 | tf_op jit(solution)/shard_map/all_gather | solution.py:13
  87.8 1.4 slice-done
  89.2 0.9 copy.56
  90.1 14.3 %while.19 = (s32[]{:T(128)}, f32[192,16]{0,1:T(8,128)S(1)}, f32[192,16]{0,1:T(8,128)S(1)}, f32[192,16,128]{2,1,0:T(8,128)S(1)}, f32[4,192,16]{1,2,0:T(8,128)}, /...) while((s32[]{:T(128)}, f32[192,16]{0,1:T(8,128)S(1)}, ...), condition=%wide.region_4.5_spmd, body=%wide.region_3.4_spmd.sunk | while | flops 1198085 | bytes 8036503 | solution.py:19
  90.1 0.7 fusion.43
  90.8 0.1 copy.114
  90.9 0.1 copy.115
  91.0 1.5 constant_dynamic-slice_fusion.2
  92.6 2.3 %fusion.44 = f32[192,16,128]{2,1,0:T(8,128)S(1)} fusion(f32[1,192,16,128]{3,1,0,2:T(8,128)S(1)} %constant_dynamic-slice_fusion.2, f32[192,16,128]{2,1,0:T(8,128)S(1)} %get-tuple-element.300, f32[192,16]{1,0:T(8,128)S(1)} %copy.114, f32[192,16]{1,0:T(8,128)S(1)} %copy.115), kind=kLoop, calls=%fused_computation.2.clone.1 | loop fusion | flops 1179648 | bytes 4743168 | tf_op jit(solution)/shard_map/while/body/eval_jaxpr/add | solution.py:27
  94.9 0.7 fusion.43
  95.6 0.1 copy.114
  95.7 0.1 copy.115
  95.8 1.5 constant_dynamic-slice_fusion.2
  97.4 2.3 %fusion.44 = f32[192,16,128]{2,1,0:T(8,128)S(1)} fusion(f32[1,192,16,128]{3,1,0,2:T(8,128)S(1)} %constant_dynamic-slice_fusion.2, f32[192,16,128]{2,1,0:T(8,128)S(1)} %get-tuple-element.300, f32[192,16]{1,0:T(8,128)S(1)} %copy.114, f32[192,16]{1,0:T(8,128)S(1)} %copy.115), kind=kLoop, calls=%fused_computation.2.clone.1 | loop fusion | flops 1179648 | bytes 4743168 | tf_op jit(solution)/shard_map/while/body/eval_jaxpr/add | solution.py:27
  99.6 0.7 fusion.43
  100.4 0.1 copy.114
  100.5 0.1 copy.115
  100.6 1.5 constant_dynamic-slice_fusion.2
  102.1 2.3 %fusion.44 = f32[192,16,128]{2,1,0:T(8,128)S(1)} fusion(f32[1,192,16,128]{3,1,0,2:T(8,128)S(1)} %constant_dynamic-slice_fusion.2, f32[192,16,128]{2,1,0:T(8,128)S(1)} %get-tuple-element.300, f32[192,16]{1,0:T(8,128)S(1)} %copy.114, f32[192,16]{1,0:T(8,128)S(1)} %copy.115), kind=kLoop, calls=%fused_computation.2.clone.1 | loop fusion | flops 1179648 | bytes 4743168 | tf_op jit(solution)/shard_map/while/body/eval_jaxpr/add | solution.py:27
  104.4 0.1 copy.60
  104.5 1.5 convolution_bitcast_fusion.2
  106.1 0.7 stack_reshape.7
  106.8 0.9 multiply_reduce_fusion
  107.7 0.1 copy.61
  107.8 1.8 fusion.9
  109.5 0.3 fusion.10
  109.8 0.1 copy.65
  109.9 0.7 pad_maximum_fusion
  110.7 0.0 all-reduce.6.cloned.1.call-update
  110.7 0.0 copy-start.7
  110.7 0.0 all-reduce.4.cloned.1.call-start
  110.7 0.4 fusion.4
  111.2 1.1 copy.109
  112.3 0.0 all-reduce.4.cloned.1.call-update
  112.3 0.6 dynamic-slice
  113.5 32.9 %all-reduce.6.cloned.1.call-done = f32[16,2,2048]{2,0,1:T(8,128)} async-done(((f32[16,2,2048]{2,0,1:T(8,128)}), f32[16,2,2048]{2,0,1:T(8,128)}) %all-reduce.6.cloned.1.call-update) | async-done | bytes 262160
  146.5 1.5 dynamic-slice_bitcast_fusion
  148.0 36.4 %all-reduce.4.cloned.1.call-done = bf16[192,2048]{1,0:T(8,128)(2,1)} async-done(((bf16[192,2048]{1,0:T(8,128)(2,1)}), bf16[192,2048]{1,0:T(8,128)(2,1)}) %all-reduce.4.cloned.1.call-update) | async-done | bytes 786448 | tf_op jit(solution)/shard_map/psum | solution.py:85
  184.4 2.1 %copy.130 = bf16[192,2048]{1,0:T(8,128)(2,1)} copy(bf16[192,2048]{1,0:T(8,128)(2,1)} %all-reduce.4.cloned.1.call-done) | data formatting | bytes 1572864
  (14 shorter events, 0.2 us)
Async XLA Ops:
  7.2 30.9 %copy-start = (bf16[192,2048]{1,0:T(8,128)(2,1)S(1)}, bf16[192,2048]{1,0:T(8,128)(2,1)}, u32[]{:S(2)}) copy-start(bf16[192,2048]{1,0:T(8,128)(2,1)} %param.8) | copy-start | bytes 2359300
  7.2 80.6 %all-gather.9.cloned.1.call-start = ((), (), s32[]{:S(2)}) async-start(), calls=%async_computation.1 | async-start | bytes 7864320 | tf_op jit(solution)/shard_map/all_gather | solution.py:13
  38.1 2.2 %copy-start.4 = (bf16[16,16,128]{2,1,0:T(8,128)(2,1)}, bf16[16,16,128]{2,1,0:T(8,128)(2,1)S(1)}, u32[]{:S(2)}) copy-start(bf16[16,16,128]{2,1,0:T(8,128)(2,1)S(1)} %reshape.54) | copy-start | bytes 196612
  38.7 3.1 %copy-start.1 = (f32[192,16,16]{0,2,1:T(8,128)}, f32[192,16,16]{0,2,1:T(8,128)S(1)}, u32[]{:S(2)}) copy-start(f32[192,16,16]{0,2,1:T(8,128)S(1)} %get-tuple-element.235) | copy-start | bytes 589828
  38.7 1.7 copy-start.6
  38.7 1.8 copy-start.2
  40.3 106.2 %all-reduce.6.cloned.1.call-start = ((), (), s32[]{:S(2)}) async-start(), calls=%async_computation.2 | async-start | bytes 524288
  87.8 1.4 slice-start
  106.0 1.7 copy-start.5
  107.8 2.2 %copy-start.3 = (f32[16,1,2048]{2,0,1:T(8,128)S(1)}, f32[16,1,2048]{2,0,1:T(8,128)}, u32[]{:S(2)}) copy-start(f32[16,1,2048]{2,0,1:T(8,128)} %stack_reshape.7) | copy-start | bytes 393220
  110.7 1.6 copy-start.7
  110.7 73.7 %all-reduce.4.cloned.1.call-start = ((), (), s32[]{:S(2)}) async-start(), calls=%async_computation | async-start | bytes 1572864 | tf_op jit(solution)/shard_map/psum | solution.py:85
Sparse Core Ops, SparseCore 0:
  40.4 47.2 all-gather.8
  110.8 35.6 all-reduce.5
  149.4 34.8 all-reduce.3
where the time goes:
time: 194 us; the launch traced here: 193 us
  waiting for transfers between devices  104 us (54%)
  blocking collectives  39.7 us (20%)
  local copies, waits for them, and re-layouts  14.8 us (8%)
  between operations  14.6 us (8%)
  other arithmetic  13.8 us (7%)
  matrix products  6.16 us (3%)
    psum x1, waiting for transfers between devices, per_device(): lax.psum(query_share.reshape(row_count, feat_width).astype(jnp.bfloat16),...  36.4 us
    all_gather x1, waiting for transfers between devices, joined(): everything = jax.tree.map(lambda part: lax.all_gather(part, axis), x)  34.3 us
    unnamed x4, waiting for transfers between devices  33 us
    all_gather x1, blocking collectives, per_device(): lax.all_gather(keys, 'seq', axis=0, tiled=True)  15.3 us
    all_gather x1, blocking collectives, per_device(): lax.all_gather(values, 'seq', axis=0, tiled=True)  13.5 us
    all_gather x2, blocking collectives, joined(): everything = jax.tree.map(lambda part: lax.all_gather(part, axis), x)  10.9 us
    add x3, other arithmetic, combine_full(): left_part[2] * left_factor[..., None]  6.79 us
    dynamic_slice x3, local copies, waits for them, and re-layouts, hop(): return combine(so_far, jax.tree.map(lambda part: part[k], everything))  4.6 us
  transfers between devices with their start and end apart: 3, of which 3 were waited for; matrix products, arithmetic and copies ran while one was open for 3% of the time, Pallas kernels for 0%

commit v1 on v0

v1 whole, which is shorter than its diff:
```python
import functools
import math

import jax
import jax.numpy as jnp
from jax import lax
from jax.experimental import pallas as pl
from jax.experimental.pallas import tpu as pltpu
from jax.sharding import PartitionSpec as P

HD = 128
SEQS = 2
MESH = pl.DeviceIdType.MESH


def each(low, high, step):
    if high - low <= 8:
        for k in range(low, high):
            step(k)
    else:
        lax.fori_loop(low, high, lambda k, c: (step(k), c)[1], 0)


def kernel(
    nsec, nseq,
    text_ref, klen_ref, q_hbm, k_ref, v_ref, g_hbm,
    qg_ref, kg_ref, vg_ref,
    q_ref, g_ref, gk, gv, kall, vall, full, part, inbox,
    local_sem, send1, recv1, send2, recv2, send3, recv3,
):
    sec = lax.axis_index("section")
    seq = lax.axis_index("seq")
    tok = k_ref.shape[0]
    rows, width = q_ref.shape
    heads = width // HD
    slab = nseq * tok
    vol = nsec * slab
    scale = 1.0 / math.sqrt(HD)

    local = [
        pltpu.make_async_copy(q_hbm, q_ref, local_sem.at[0]),
        pltpu.make_async_copy(g_hbm, g_ref, local_sem.at[1]),
        pltpu.make_async_copy(k_ref, gk.at[sec * nseq + seq], local_sem.at[2]),
        pltpu.make_async_copy(v_ref, gv.at[sec * nseq + seq], local_sem.at[3]),
    ]
    for copy in local:
        copy.start()

    barrier = pltpu.get_barrier_semaphore()

    def greet(axis, me, count):
        def one(k):
            pl.semaphore_signal(
                barrier, inc=1, device_id={axis: lax.rem(me + k, count)}, device_id_type=MESH
            )
        each(1, count, one)

    greet("seq", seq, nseq)
    greet("section", sec, nsec)
    pl.semaphore_wait(barrier, nseq + nsec - 2)

    def along_seq(k, which, src, dst):
        return pltpu.make_async_remote_copy(
            src_ref=src, dst_ref=dst.at[sec * nseq + seq],
            send_sem=send1.at[which, k], recv_sem=recv1.at[which, k],
            device_id={"seq": lax.rem(seq + k, nseq)}, device_id_type=MESH,
        )

    def along_section(k, p, which, src, dst):
        slot = sec * nseq + lax.rem(seq + nseq - k, nseq)
        return pltpu.make_async_remote_copy(
            src_ref=src, dst_ref=dst.at[slot],
            send_sem=send2.at[which, p, k], recv_sem=recv2.at[which, p, k],
            device_id={"section": lax.rem(sec + p, nsec)}, device_id_type=MESH,
        )

    pairs = ((0, k_ref, gk), (1, v_ref, gv))

    def start1(k):
        for which, src, dst in pairs:
            along_seq(k, which, src, dst).start()

    each(1, nseq, start1)
    for p in range(1, nsec):
        for which, src, dst in pairs:
            along_section(0, p, which, src, dst).start()

    def forward(k):
        slot = sec * nseq + lax.rem(seq + nseq - k, nseq)
        for which, src, dst in pairs:
            along_seq(k, which, src, dst).wait_recv()
            for p in range(1, nsec):
                along_section(k, p, which, dst.at[slot], dst).start()

    each(1, nseq, forward)

    def arrive(k):
        for which, src, dst in pairs:
            for p in range(1, nsec):
                along_section(k, p, which, src, dst).wait_recv()

    each(0, nseq, arrive)
    for copy in local:
        copy.wait()

    def spread(j):
        for src, dst in ((gk, kall), (gv, vall)):
            dst[j, 0:tok, :] = src[2 * j].astype(jnp.float32)
            dst[j, tok:2 * tok, :] = src[2 * j + 1].astype(jnp.float32)

    each(0, nsec * nseq // 2, spread)

    length = rows * nseq // SEQS
    position = seq * rows + lax.broadcasted_iota(jnp.int32, (1, rows), 1)
    alive = jnp.zeros((1, rows), jnp.int32)
    for s in range(SEQS):
        inside = (position >= s * length) & (position < s * length + text_ref[s])
        alive = jnp.where(inside, 1, alive)
    alive = alive > 0
    token = lax.broadcasted_iota(jnp.int32, (vol, rows), 0)
    limit = jnp.zeros((vol, rows), jnp.int32)
    for s in range(nsec):
        limit = jnp.where(token >= s * slab, s * slab + klen_ref[s], limit)
    live = token < limit

    def head(h):
        cols = pl.ds(pl.multiple_of(h * HD, HD), HD)
        q = q_ref[:, cols]
        g = g_ref[:, cols]
        key = kall[:, :, cols].reshape(vol, HD).astype(jnp.bfloat16)
        value = vall[:, :, cols].reshape(vol, HD).astype(jnp.bfloat16)
        nt = (((1,), (1,)), ((), ()))
        scores = lax.dot_general(key, q, nt, preferred_element_type=jnp.float32) * scale
        prob_grad = lax.dot_general(value, g, nt, preferred_element_type=jnp.float32)
        scores = jnp.where(live, scores, jnp.float32(-1e30))
        expo = jnp.exp(scores - jnp.max(scores, axis=0, keepdims=True))
        total = jnp.sum(expo, axis=0, keepdims=True)
        probs = expo * jnp.where(alive, 1.0 / total, 0.0)
        row_dot = jnp.sum(probs * prob_grad, axis=0, keepdims=True)
        score_grad = (probs * (prob_grad - row_dot)).astype(jnp.bfloat16)
        tn = (((0,), (0,)), ((), ()))
        qg = lax.dot_general(score_grad, key, tn, preferred_element_type=jnp.float32) * scale
        qg_ref[:, cols] = qg.astype(jnp.bfloat16)
        nn = (((1,), (0,)), ((), ()))
        full[0, :, cols] = (
            lax.dot_general(score_grad, q, nn, preferred_element_type=jnp.float32) * scale
        )
        full[1, :, cols] = lax.dot_general(
            probs.astype(jnp.bfloat16), g, nn, preferred_element_type=jnp.float32
        )

    unroll = 4 if heads % 4 == 0 and vol <= 128 else 1

    def several(i, c):
        for u in range(unroll):
            head(i * unroll + u)
        return c

    lax.fori_loop(0, heads // unroll, several, 0)

    def gather_rows(j):
        at = pl.multiple_of(sec * slab + j * 2 * tok, 2 * tok)
        for which in range(2):
            both = full[which, pl.ds(at, 2 * tok), :]
            part[2 * j, which] = both[0:tok]
            part[2 * j + 1, which] = both[tok:2 * tok]

    each(0, nseq // 2, gather_rows)

    def share(k):
        dest = lax.rem(seq + k, nseq)
        return pltpu.make_async_remote_copy(
            src_ref=part.at[dest], dst_ref=inbox.at[k],
            send_sem=send3.at[k], recv_sem=recv3.at[k],
            device_id={"seq": dest}, device_id_type=MESH,
        )

    each(1, nseq, lambda k: share(k).start())
    kg_ref[...] = part[seq, 0]
    vg_ref[...] = part[seq, 1]

    def add(k):
        share(k).wait_recv()
        kg_ref[...] += inbox[k, 0]
        vg_ref[...] += inbox[k, 1]

    each(1, nseq, add)

    def drain(k):
        share(k).wait_send()
        for which, src, dst in pairs:
            along_seq(k, which, src, dst).wait_send()

    each(1, nseq, drain)

    def drain2(k):
        for which, src, dst in pairs:
            for p in range(1, nsec):
                along_section(k, p, which, src, dst).wait_send()

    each(0, nseq, drain2)


def solution(mesh):
    nsec, nseq = mesh.shape["section"], mesh.shape["seq"]

    def per_device(queries, keys, values, out_grad, text_len, key_len):
        rows, width = queries.shape
        tok = keys.shape[0]
        slots = nsec * nseq
        vmem = pl.BlockSpec(memory_space=pltpu.VMEM)
        smem = pl.BlockSpec(memory_space=pltpu.SMEM)
        hbm = pl.BlockSpec(memory_space=pl.ANY)
        dma = pltpu.SemaphoreType.DMA
        return pl.pallas_call(
            functools.partial(kernel, nsec, nseq),
            out_shape=(
                jax.ShapeDtypeStruct((rows, width), jnp.bfloat16),
                jax.ShapeDtypeStruct((tok, width), jnp.float32),
                jax.ShapeDtypeStruct((tok, width), jnp.float32),
            ),
            in_specs=[smem, smem, hbm, vmem, vmem, hbm],
            out_specs=(vmem, vmem, vmem),
            scratch_shapes=[
                pltpu.VMEM((rows, width), jnp.bfloat16),
                pltpu.VMEM((rows, width), jnp.bfloat16),
                pltpu.VMEM((slots, tok, width), jnp.bfloat16),
                pltpu.VMEM((slots, tok, width), jnp.bfloat16),
                pltpu.VMEM((slots // 2, 2 * tok, width), jnp.float32),
                pltpu.VMEM((slots // 2, 2 * tok, width), jnp.float32),
                pltpu.VMEM((2, slots * tok, width), jnp.float32),
                pltpu.VMEM((nseq, 2, tok, width), jnp.float32),
                pltpu.VMEM((nseq, 2, tok, width), jnp.float32),
                dma((4,)),
                dma((2, nseq)), dma((2, nseq)),
                dma((2, nsec, nseq)), dma((2, nsec, nseq)),
                dma((nseq,)), dma((nseq,)),
            ],
            compiler_params=pltpu.CompilerParams(
                collective_id=0, has_side_effects=True, vmem_limit_bytes=64000 * 1024
            ),
        )(text_len, key_len, queries, keys, values, out_grad)

    in_specs = (
        P("seq", "tp"),
        P(("section", "seq"), "tp"),
        P(("section", "seq"), "tp"),
        P("seq", "tp"),
        P(),
        P(),
    )
    out_specs = (P("seq", "tp"), P(("section", "seq"), "tp"), P(("section", "seq"), "tp"))
    return jax.shard_map(
        per_device, mesh=mesh, in_specs=in_specs, out_specs=out_specs, check_vma=False
    )
```

time: 194 us -> 32.8 us (0.17)
  waiting for transfers between devices: 104 us -> 0 us
  blocking collectives: 39.7 us -> 0 us
  Pallas kernels: 0 us -> 28.4 us
  between operations: 14.6 us -> 0.65 us
  other arithmetic: 13.8 us -> 0 us
  local copies, waits for them, and re-layouts: 14.8 us -> 3.48 us
  matrix products: 6.16 us -> 0 us
    all_gather x4 -> x0, blocking collectives: 39.7 us -> none  [the longest x1 15.3 us: per_device(): lax.all_gather(keys, 'seq', axis=0, tiled=True)]
    psum x1 -> x0, waiting for transfers between devices: 36.4 us -> none  [per_device(): lax.psum(query_share.reshape(row_count, feat_width).astype(jnp.bfloat16),...]
    all_gather x1 -> x0, waiting for transfers between devices: 34.3 us -> none  [joined(): everything = jax.tree.map(lambda part: lax.all_gather(part, axis), x)]
    unnamed x4 -> x0, waiting for transfers between devices: 33 us -> none
    pallas_call x0 -> x1, Pallas kernels: none -> 28.4 us  [per_device(): pl.pallas_call(functools.partial(kernel, nsec, nseq), out_shape=(jax.Shap...]
    add x6 -> x0, other arithmetic: 9.02 us -> none  [the longest x3 6.79 us: combine_full(): left_part[2] * left_factor[..., None]]
    dot_general x6 -> x0, matrix products: 6.16 us -> none  [the longest x1 1.76 us: per_device(): jnp.einsum('qhd,khd->qhk', grad_heads, value_heads, preferred_element_typ...]
    dynamic_slice x3 -> x0, local copies, waits for them, and re-layouts: 4.6 us -> none  [hop(): return combine(so_far, jax.tree.map(lambda part: part[k], everything))]
  transfers between devices with their start and end apart: 3 -> 0, of which waited for: 3 -> 0; matrix products, arithmetic and copies ran while one was open for 3% -> 0% of each run, Pallas kernels for 0% -> 0%
where the time goes in v1:
time: 32.8 us; the launch traced here: 32.5 us
  Pallas kernels  28.4 us (87%)
  local copies, waits for them, and re-layouts  3.48 us (11%)
  between operations  0.65 us (2%)
    pallas_call x1, Pallas kernels, per_device(): pl.pallas_call(functools.partial(kernel, nsec, nseq), out_shape=(jax.Shap...  28.4 us
    unnamed x7, local copies, waits for them, and re-layouts  3.48 us

profile of v1, /device:TPU:0, one launch (start us, length us, event | category | flops | bytes accessed | tf_op | source)
XLA Modules:
  0.0 32.5 jit_solution(4080698332895151726)
XLA Ops:
  0.6 28.4 %shard_map.85 = (bf16[192,2048]{1,0:T(8,128)(2,1)}, f32[4,2048]{1,0:T(4,128)}, f32[4,2048]{1,0:T(4,128)}) custom-call(s32[2]{0:T(128)} %text_ref.1, s32[4]{0:T(128)} %klen_ref.1, bf16[192,2048]{1,0:T(8,128)(2,1)} %q_hbm.1, bf16[4,2048]{1,0:T(4,128)(2,1)} %k_ref.1, bf16[4,2048]{1,0:T(4,128)(2,1)} %v_ref.1, bf16[192,2048]{1,0:T(8,128)(2,1)} %g_hbm.1), custom_call_target="tpu_custom_call" | custom-call | tf_op jit(solution)/shard_map/pallas_call | solution.py:215
  29.0 0.0 copy-start.1
  29.0 2.1 %copy.12 = bf16[192,2048]{1,0:T(8,128)(2,1)} copy(bf16[192,2048]{1,0:T(8,128)(2,1)} %get-tuple-element.6) | data formatting | bytes 1572864
  31.1 0.0 copy-done.1
  31.1 0.0 copy-start
  31.1 0.6 %copy.13 = f32[4,2048]{1,0:T(4,128)} copy(f32[4,2048]{1,0:T(4,128)S(1)} %copy-done.1) | data formatting | bytes 65536
  31.8 0.2 copy-done
  31.9 0.6 %copy.14 = f32[4,2048]{1,0:T(4,128)} copy(f32[4,2048]{1,0:T(4,128)S(1)} %copy-done) | data formatting | bytes 65536
Async XLA Ops:
  29.0 2.1 %copy-start.1 = (f32[4,2048]{1,0:T(4,128)S(1)}, f32[4,2048]{1,0:T(4,128)}, u32[]{:S(2)}) copy-start(f32[4,2048]{1,0:T(4,128)} %get-tuple-element.7) | copy-start | bytes 98308
  31.1 0.8 %copy-start = (f32[4,2048]{1,0:T(4,128)S(1)}, f32[4,2048]{1,0:T(4,128)}, u32[]{:S(2)}) copy-start(f32[4,2048]{1,0:T(4,128)} %get-tuple-element.8) | copy-start | bytes 98308

commit v2 on v1

--- a/solution.py
+++ b/solution.py
@@ -25,7 +25,7 @@
     nsec, nseq,
     text_ref, klen_ref, q_hbm, k_ref, v_ref, g_hbm,
     qg_ref, kg_ref, vg_ref,
-    q_ref, g_ref, gk, gv, kall, vall, full, part, inbox,
+    q_ref, g_ref, gk, gv, kall, vall, full, mine, part, inbox,
     local_sem, send1, recv1, send2, recv2, send3, recv3,
 ):
     sec = lax.axis_index("section")
@@ -66,12 +66,18 @@
             device_id={"seq": lax.rem(seq + k, nseq)}, device_id_type=MESH,
         )
 
+    twin = sec + 1 - 2 * lax.rem(sec, 2)
+    across = lax.rem(sec + 2, 4)
+
+    def slot_of(owner, k):
+        return owner * nseq + lax.rem(seq + nseq - k, nseq)
+
     def along_section(k, p, which, src, dst):
-        slot = sec * nseq + lax.rem(seq + nseq - k, nseq)
+        owner = across if p == 2 else sec
         return pltpu.make_async_remote_copy(
-            src_ref=src, dst_ref=dst.at[slot],
+            src_ref=src, dst_ref=dst.at[slot_of(owner, k)],
             send_sem=send2.at[which, p, k], recv_sem=recv2.at[which, p, k],
-            device_id={"section": lax.rem(sec + p, nsec)}, device_id_type=MESH,
+            device_id={"section": across if p == 0 else twin}, device_id_type=MESH,
         )
 
     pairs = ((0, k_ref, gk), (1, v_ref, gv))
@@ -81,22 +87,28 @@
             along_seq(k, which, src, dst).start()
 
     each(1, nseq, start1)
-    for p in range(1, nsec):
+    for p in range(2):
         for which, src, dst in pairs:
             along_section(0, p, which, src, dst).start()
 
+    def relay(k):
+        for which, src, dst in pairs:
+            along_section(k, 0, which, src, dst).wait_recv()
+            along_section(k, 2, which, dst.at[slot_of(across, k)], dst).start()
+
     def forward(k):
-        slot = sec * nseq + lax.rem(seq + nseq - k, nseq)
         for which, src, dst in pairs:
             along_seq(k, which, src, dst).wait_recv()
-            for p in range(1, nsec):
-                along_section(k, p, which, dst.at[slot], dst).start()
+            for p in range(2):
+                along_section(k, p, which, dst.at[slot_of(sec, k)], dst).start()
+        relay(k - 1)
 
     each(1, nseq, forward)
+    relay(nseq - 1)
 
     def arrive(k):
         for which, src, dst in pairs:
-            for p in range(1, nsec):
+            for p in range(1, 3):
                 along_section(k, p, which, src, dst).wait_recv()
 
     each(0, nseq, arrive)
@@ -149,45 +161,54 @@
             probs.astype(jnp.bfloat16), g, nn, preferred_element_type=jnp.float32
         )
 
-    unroll = 4 if heads % 4 == 0 and vol <= 128 else 1
-
-    def several(i, c):
-        for u in range(unroll):
-            head(i * unroll + u)
-        return c
-
-    lax.fori_loop(0, heads // unroll, several, 0)
-
-    def gather_rows(j):
-        at = pl.multiple_of(sec * slab + j * 2 * tok, 2 * tok)
-        for which in range(2):
-            both = full[which, pl.ds(at, 2 * tok), :]
-            part[2 * j, which] = both[0:tok]
-            part[2 * j + 1, which] = both[tok:2 * tok]
-
-    each(0, nseq // 2, gather_rows)
-
-    def share(k):
+    groups = 4
+    per_group = heads // groups
+    span = width // groups
+
+    def share(k, group):
         dest = lax.rem(seq + k, nseq)
+        cols = pl.ds(group * span, span)
         return pltpu.make_async_remote_copy(
-            src_ref=part.at[dest], dst_ref=inbox.at[k],
-            send_sem=send3.at[k], recv_sem=recv3.at[k],
+            src_ref=part.at[dest, :, :, cols], dst_ref=inbox.at[k, :, :, cols],
+            send_sem=send3.at[group, k], recv_sem=recv3.at[group, k],
             device_id={"seq": dest}, device_id_type=MESH,
         )
 
-    each(1, nseq, lambda k: share(k).start())
-    kg_ref[...] = part[seq, 0]
-    vg_ref[...] = part[seq, 1]
+    for group in range(groups):
+        if vol <= 128:
+            for u in range(per_group):
+                head(group * per_group + u)
+        else:
+            lax.fori_loop(0, per_group, lambda u, c: (head(group * per_group + u), c)[1], 0)
+        cols = pl.ds(group * span, span)
+
+        def gather_rows(j):
+            at = pl.multiple_of(sec * slab + j * 2 * tok, 2 * tok)
+            for which in range(2):
+                both = full[which, pl.ds(at, 2 * tok), cols]
+                for half in range(2):
+                    piece = both[half * tok:(half + 1) * tok]
+                    mine[2 * j + half, which, :, cols] = piece
+                    part[2 * j + half, which, :, cols] = piece.astype(jnp.bfloat16)
+
+        each(0, nseq // 2, gather_rows)
+        if group > 0:
+            each(1, nseq, lambda k: share(k, group - 1).start())
+    kg_ref[...] = mine[seq, 0]
+    vg_ref[...] = mine[seq, 1]
+    each(1, nseq, lambda k: share(k, groups - 1).start())
 
     def add(k):
-        share(k).wait_recv()
-        kg_ref[...] += inbox[k, 0]
-        vg_ref[...] += inbox[k, 1]
+        for group in range(groups):
+            share(k, group).wait_recv()
+        kg_ref[...] += inbox[k, 0].astype(jnp.float32)
+        vg_ref[...] += inbox[k, 1].astype(jnp.float32)
 
     each(1, nseq, add)
 
     def drain(k):
-        share(k).wait_send()
+        for group in range(groups):
+            share(k, group).wait_send()
         for which, src, dst in pairs:
             along_seq(k, which, src, dst).wait_send()
 
@@ -195,7 +216,7 @@
 
     def drain2(k):
         for which, src, dst in pairs:
-            for p in range(1, nsec):
+            for p in range(3):
                 along_section(k, p, which, src, dst).wait_send()
 
     each(0, nseq, drain2)
@@ -230,11 +251,12 @@
                 pltpu.VMEM((slots // 2, 2 * tok, width), jnp.float32),
                 pltpu.VMEM((2, slots * tok, width), jnp.float32),
                 pltpu.VMEM((nseq, 2, tok, width), jnp.float32),
-                pltpu.VMEM((nseq, 2, tok, width), jnp.float32),
+                pltpu.VMEM((nseq, 2, tok, width), jnp.bfloat16),
+                pltpu.VMEM((nseq, 2, tok, width), jnp.bfloat16),
                 dma((4,)),
                 dma((2, nseq)), dma((2, nseq)),
                 dma((2, nsec, nseq)), dma((2, nsec, nseq)),
-                dma((nseq,)), dma((nseq,)),
+                dma((4, nseq)), dma((4, nseq)),
             ],
             compiler_params=pltpu.CompilerParams(
                 collective_id=0, has_side_effects=True, vmem_limit_bytes=64000 * 1024

time: 32.8 us -> 30.5 us (0.930)
  Pallas kernels: 28.4 us -> 26.1 us
    pallas_call x1, Pallas kernels: 28.4 us -> 26.1 us  [per_device(): pl.pallas_call(functools.partial(kernel, nsec, nseq), out_shape=(jax.Shap...]
where the time goes in v2:
time: 30.5 us; the launch traced here: 30.2 us
  Pallas kernels  26.1 us (86%)
  local copies, waits for them, and re-layouts  3.48 us (11%)
  between operations  0.65 us (2%)
    pallas_call x1, Pallas kernels, per_device(): pl.pallas_call(functools.partial(kernel, nsec, nseq), out_shape=(jax.Shap...  26.1 us
    unnamed x7, local copies, waits for them, and re-layouts  3.48 us

profile of v2, /device:TPU:0, one launch (start us, length us, event | category | flops | bytes accessed | tf_op | source)
XLA Modules:
  0.0 30.2 jit_solution(2462820145706407792)
XLA Ops:
  0.6 26.1 %shard_map.85 = (bf16[192,2048]{1,0:T(8,128)(2,1)}, f32[4,2048]{1,0:T(4,128)}, f32[4,2048]{1,0:T(4,128)}) custom-call(s32[2]{0:T(128)} %text_ref.1, s32[4]{0:T(128)} %klen_ref.1, bf16[192,2048]{1,0:T(8,128)(2,1)} %q_hbm.1, bf16[4,2048]{1,0:T(4,128)(2,1)} %k_ref.1, bf16[4,2048]{1,0:T(4,128)(2,1)} %v_ref.1, bf16[192,2048]{1,0:T(8,128)(2,1)} %g_hbm.1), custom_call_target="tpu_custom_call" | custom-call | tf_op jit(solution)/shard_map/pallas_call | solution.py:236
  26.7 0.0 copy-start.1
  26.7 2.1 %copy.12 = bf16[192,2048]{1,0:T(8,128)(2,1)} copy(bf16[192,2048]{1,0:T(8,128)(2,1)} %get-tuple-element.6) | data formatting | bytes 1572864
  28.8 0.0 copy-done.1
  28.8 0.0 copy-start
  28.8 0.6 %copy.13 = f32[4,2048]{1,0:T(4,128)} copy(f32[4,2048]{1,0:T(4,128)S(1)} %copy-done.1) | data formatting | bytes 65536
  29.5 0.2 copy-done
  29.6 0.6 %copy.14 = f32[4,2048]{1,0:T(4,128)} copy(f32[4,2048]{1,0:T(4,128)S(1)} %copy-done) | data formatting | bytes 65536
Async XLA Ops:
  26.7 2.1 %copy-start.1 = (f32[4,2048]{1,0:T(4,128)S(1)}, f32[4,2048]{1,0:T(4,128)}, u32[]{:S(2)}) copy-start(f32[4,2048]{1,0:T(4,128)} %get-tuple-element.7) | copy-start | bytes 98308
  28.8 0.8 %copy-start = (f32[4,2048]{1,0:T(4,128)S(1)}, f32[4,2048]{1,0:T(4,128)}, u32[]{:S(2)}) copy-start(f32[4,2048]{1,0:T(4,128)} %get-tuple-element.8) | copy-start | bytes 98308
